TPU v7x, 32 devices: a whole 2x2x4 slice. The times are simulated.
32 devices in a mesh: dp: 8 (over y, x, core), seq: 4 (over z).
Axes of the slice: x: 2, y: 2, z: 4, core: 2. Of those that a mesh axis runs over, the one named last changes fastest.
Arguments:
- tokens: bfloat16 [2, 8, 2048, 768], P(None, 'dp', 'seq'), may hold values from -6 to 6
- seq_lengths: int32 [2, 8], P(None, 'dp'), may hold values from 512 to 2048, as said below
- query_weight: bfloat16 [768, 768], P(('dp', 'seq')), may hold values from -0.21875 to 0.21875
- query_bias: bfloat16 [768], P(('dp', 'seq')), may hold values from -3 to 3
- key_weight: bfloat16 [768, 768], P(('dp', 'seq')), may hold values from -0.21875 to 0.21875
- key_bias: bfloat16 [768], P(('dp', 'seq')), may hold values from -3 to 3
- value_weight: bfloat16 [768, 768], P(('dp', 'seq')), may hold values from -0.21875 to 0.21875
- value_bias: bfloat16 [768], P(('dp', 'seq')), may hold values from -3 to 3
- output_weight: bfloat16 [768, 768], P(('dp', 'seq')), may hold values from -1.25 to 1.25
- output_bias: bfloat16 [768], P(('dp', 'seq')), may hold values from -3 to 3
- gain_first: bfloat16 [768], P(('dp', 'seq')), may hold values from 0.5 to 1.5
- shift_first: bfloat16 [768], P(('dp', 'seq')), may hold values from -3 to 3
- inner_weight: bfloat16 [768, 3072], P(('dp', 'seq')), may hold values from -0.21875 to 0.21875
- inner_bias: bfloat16 [3072], P(('dp', 'seq')), may hold values from -3 to 3
- outer_weight: bfloat16 [3072, 768], P(('dp', 'seq')), may hold values from -0.109375 to 0.109375
- outer_bias: bfloat16 [768], P(('dp', 'seq')), may hold values from -3 to 3
- gain_second: bfloat16 [768], P(('dp', 'seq')), may hold values from 0.5 to 1.5
- shift_second: bfloat16 [768], P(('dp', 'seq')), may hold values from -3 to 3
- cotangent: bfloat16 [2, 8, 2048, 768], P(None, 'dp', 'seq'), may hold values from -6 to 6
Outputs:
- layer_out: bfloat16 [2, 8, 2048, 768], P(None, 'dp', 'seq')
- grad_tokens: float32 [2, 8, 2048, 768], P(None, 'dp', 'seq')
- grad_query_weight: float32 [768, 768], P(('dp', 'seq'))
- grad_query_bias: float32 [768], P(('dp', 'seq'))
- grad_key_weight: float32 [768, 768], P(('dp', 'seq'))
- grad_key_bias: float32 [768], P(('dp', 'seq'))
- grad_value_weight: float32 [768, 768], P(('dp', 'seq'))
- grad_value_bias: float32 [768], P(('dp', 'seq'))
- grad_output_weight: float32 [768, 768], P(('dp', 'seq'))
- grad_output_bias: float32 [768], P(('dp', 'seq'))
- grad_gain_first: float32 [768], P(('dp', 'seq'))
- grad_shift_first: float32 [768], P(('dp', 'seq'))
- grad_inner_weight: float32 [768, 3072], P(('dp', 'seq'))
- grad_inner_bias: float32 [3072], P(('dp', 'seq'))
- grad_outer_weight: float32 [3072, 768], P(('dp', 'seq'))
- grad_outer_bias: float32 [768], P(('dp', 'seq'))
- grad_gain_second: float32 [768], P(('dp', 'seq'))
- grad_shift_second: float32 [768], P(('dp', 'seq'))
Inputs may be any that keep to these rules, and one draw needn't show every extreme that they name: `seq_lengths`: in every micro-batch some sequence has exactly 2048 valid positions; positions at or past a sequence's length are padding.
All inputs are finite; a program needn't handle non-finite values.
Results may differ from a plain program's by a relative error of at most 0.014.
Values may be sent and summed in bfloat16 or wider, within the bound.
No kernel may reach another device: no remote copies, remote signals or barrier semaphores. Data moves between devices by JAX's collectives and lax.ppermute only.
A program may use at most 192 MiB of HBM per device.

v0:
```python
import math
import jax
import jax.numpy as jnp
from jax import lax
from jax.sharding import PartitionSpec as P

H = 12
HD = 64
BLOCK = 512
NORM_EPS = 1e-05
HALF_TURN = math.pi / 2


def layer_norm(values, norm_gain, norm_shift):
    center = values - jnp.mean(values, axis=-1, keepdims=True)
    spread = jnp.mean(center * center, axis=-1, keepdims=True)
    return center * lax.rsqrt(spread + NORM_EPS) * norm_gain + norm_shift


def reweight(places, limit):
    angle = HALF_TURN * places[:, None] / limit[None, :]
    live = (places[:, None] < limit[None, :]).astype(jnp.float32)
    return (jnp.cos(angle) * live, jnp.sin(angle) * live)


def attention(queries, key_rows, values, lengths, offset, initial):
    total_rows, head_count, head_size = queries.shape
    block_rows = min(BLOCK, total_rows)
    block_count = total_rows // block_rows
    limit = lengths.astype(jnp.float32)
    causal = jnp.tril(jnp.ones((block_rows, block_rows), jnp.float32))
    highest = lax.Precision.HIGHEST

    def attend(state_now, inputs):
        sum_cos, sum_sin, norm_cos, norm_sin = state_now
        query_blk, key_blk, value_blk, block_index = inputs
        places = (offset + block_index * block_rows + jnp.arange(block_rows)).astype(jnp.float32)
        weight_cos, weight_sin = reweight(places, limit)
        query_relu = jax.nn.relu(query_blk)
        key_relu = jax.nn.relu(key_blk)
        query_cos = query_relu * weight_cos[:, :, None]
        query_sin = query_relu * weight_sin[:, :, None]
        key_cos = key_relu * weight_cos[:, :, None]
        key_sin = key_relu * weight_sin[:, :, None]
        scores = jnp.einsum("igd,jgd->gij", query_cos, key_cos, precision=highest)
        scores = scores + jnp.einsum("igd,jgd->gij", query_sin, key_sin, precision=highest)
        scores = scores * causal[None, :, :]
        numer = jnp.einsum("gij,jge->ige", scores, value_blk, precision=highest)
        numer = numer + jnp.einsum("igd,gde->ige", query_cos, sum_cos, precision=highest)
        numer = numer + jnp.einsum("igd,gde->ige", query_sin, sum_sin, precision=highest)
        denom = jnp.sum(scores, axis=2).T
        denom = denom + jnp.einsum("igd,gd->ig", query_cos, norm_cos, precision=highest)
        denom = denom + jnp.einsum("igd,gd->ig", query_sin, norm_sin, precision=highest)
        output = numer / jnp.maximum(denom, 1.0)[:, :, None]
        sum_cos = sum_cos + jnp.einsum("jgd,jge->gde", key_cos, value_blk, precision=highest)
        sum_sin = sum_sin + jnp.einsum("jgd,jge->gde", key_sin, value_blk, precision=highest)
        norm_cos = norm_cos + jnp.sum(key_cos, axis=0)
        norm_sin = norm_sin + jnp.sum(key_sin, axis=0)
        return ((sum_cos, sum_sin, norm_cos, norm_sin), output)

    stacked = (
        queries.reshape(block_count, block_rows, head_count, head_size),
        key_rows.reshape(block_count, block_rows, head_count, head_size),
        values.reshape(block_count, block_rows, head_count, head_size),
        jnp.arange(block_count),
    )
    final_state, outputs = lax.scan(jax.checkpoint(attend), initial, stacked)
    return outputs.reshape(total_rows, head_count, head_size)


def make_state(head_count):
    return (
        jnp.zeros((head_count, HD, HD), jnp.float32),
        jnp.zeros((head_count, HD, HD), jnp.float32),
        jnp.zeros((head_count, HD), jnp.float32),
        jnp.zeros((head_count, HD), jnp.float32),
    )


def head_view(packed):
    return packed.astype(jnp.float32)


def per_device(
    tokens,
    seq_lengths,
    query_weight,
    query_bias,
    key_weight,
    key_bias,
    value_weight,
    value_bias,
    output_weight,
    output_bias,
    gain_first,
    shift_first,
    inner_weight,
    inner_bias,
    outer_weight,
    outer_bias,
    gain_second,
    shift_second,
    cotangent,
):
    seq_count = lax.axis_size("seq")
    micro_count, seqs_here, shard_rows, width = tokens.shape
    item_count = seqs_here * H
    item_share = item_count // seq_count
    seq_place = lax.axis_index("seq")
    token_count = seqs_here * shard_rows
    item_index = seq_place * item_share + jnp.arange(item_share)
    head_owner = item_index // H
    owner_match = head_owner[:, None] == jnp.arange(seqs_here)[None, :]
    totals = None
    layer_rows = []
    input_grads = []
    for batch_index in range(micro_count):
        weights_now = (
            lax.all_gather(query_weight, ("dp", "seq"), axis=0, tiled=True),
            lax.all_gather(query_bias, ("dp", "seq"), axis=0, tiled=True),
            lax.all_gather(key_weight, ("dp", "seq"), axis=0, tiled=True),
            lax.all_gather(key_bias, ("dp", "seq"), axis=0, tiled=True),
            lax.all_gather(value_weight, ("dp", "seq"), axis=0, tiled=True),
            lax.all_gather(value_bias, ("dp", "seq"), axis=0, tiled=True),
            lax.all_gather(output_weight, ("dp", "seq"), axis=0, tiled=True),
            lax.all_gather(output_bias, ("dp", "seq"), axis=0, tiled=True),
            lax.all_gather(gain_first, ("dp", "seq"), axis=0, tiled=True),
            lax.all_gather(shift_first, ("dp", "seq"), axis=0, tiled=True),
            lax.all_gather(inner_weight, ("dp", "seq"), axis=0, tiled=True),
            lax.all_gather(inner_bias, ("dp", "seq"), axis=0, tiled=True),
            lax.all_gather(outer_weight, ("dp", "seq"), axis=0, tiled=True),
            lax.all_gather(outer_bias, ("dp", "seq"), axis=0, tiled=True),
            lax.all_gather(gain_second, ("dp", "seq"), axis=0, tiled=True),
            lax.all_gather(shift_second, ("dp", "seq"), axis=0, tiled=True),
        )
        (
            w_query,
            b_query,
            w_key,
            b_key,
            w_value,
            b_value,
            w_output,
            b_output,
            gain_one,
            shift_one,
            w_inner,
            b_inner,
            w_outer,
            b_outer,
            gain_two,
            shift_two,
        ) = weights_now
        lengths_now = seq_lengths[batch_index]
        head_lengths = jnp.sum(jnp.where(owner_match, lengths_now[None, :], 0), axis=1)
        token_now = tokens[batch_index]

        def project(weight_full, bias_full):
            product = jnp.einsum(
                "srd,de->rse", token_now, weight_full, preferred_element_type=jnp.float32
            )
            return (product + bias_full.astype(jnp.float32)).astype(jnp.bfloat16)

        query_low = project(w_query, b_query)
        key_low = project(w_key, b_key)
        value_low = project(w_value, b_value)
        moved = (
            lax.all_to_all(
                query_low.reshape(shard_rows, item_count, HD),
                "seq",
                split_axis=1,
                concat_axis=0,
                tiled=True,
            ),
            lax.all_to_all(
                key_low.reshape(shard_rows, item_count, HD),
                "seq",
                split_axis=1,
                concat_axis=0,
                tiled=True,
            ),
            lax.all_to_all(
                value_low.reshape(shard_rows, item_count, HD),
                "seq",
                split_axis=1,
                concat_axis=0,
                tiled=True,
            ),
        )
        zero_state = make_state(item_share)

        def core_heads(query_in, key_in, value_in):
            return attention(query_in, key_in, value_in, head_lengths, 0, zero_state)

        mixed_heads, attention_pull = jax.vjp(
            core_heads, head_view(moved[0]), head_view(moved[1]), head_view(moved[2])
        )
        mixed_send = mixed_heads.astype(jnp.bfloat16)
        mixed_low = lax.all_to_all(
            mixed_send, "seq", split_axis=0, concat_axis=1, tiled=True
        ).reshape(shard_rows, seqs_here, width)
        attended = jnp.einsum(
            "rse,ef->srf", mixed_low, w_output, preferred_element_type=jnp.float32
        )
        attended = attended + b_output.astype(jnp.float32)
        resid_one = token_now.astype(jnp.float32) + attended
        first, norm_one_pull = jax.vjp(
            layer_norm, resid_one, gain_one.astype(jnp.float32), shift_one.astype(jnp.float32)
        )
        first_flat = first.reshape(token_count, width)
        first_low = first_flat.astype(jnp.bfloat16)
        inner = jnp.dot(first_low, w_inner, preferred_element_type=jnp.float32) + b_inner.astype(
            jnp.float32
        )
        hidden_full, gelu_pull = jax.vjp(jax.nn.gelu, inner)
        hidden = hidden_full.astype(jnp.bfloat16)
        outer = jnp.dot(hidden, w_outer, preferred_element_type=jnp.float32) + b_outer.astype(
            jnp.float32
        )
        final, norm_two_pull = jax.vjp(
            layer_norm,
            first_flat + outer,
            gain_two.astype(jnp.float32),
            shift_two.astype(jnp.float32),
        )
        layer_rows.append(final.astype(jnp.bfloat16).reshape(seqs_here, shard_rows, width))
        grad_final = cotangent[batch_index].astype(jnp.float32).reshape(token_count, width)
        d_second, grad_gain_two, grad_shift_two = norm_two_pull(grad_final)
        d_outer = d_second.astype(jnp.bfloat16)
        grad_w_outer = jnp.einsum("nf,nd->fd", hidden, d_outer, preferred_element_type=jnp.float32)
        grad_b_outer = jnp.sum(d_outer, axis=0, dtype=jnp.float32)
        d_hidden = jnp.einsum("nd,fd->nf", d_outer, w_outer, preferred_element_type=jnp.float32)
        (d_inner_full,) = gelu_pull(d_hidden)
        d_inner = d_inner_full.astype(jnp.bfloat16)
        grad_w_inner = jnp.einsum(
            "nd,nf->df", first_low, d_inner, preferred_element_type=jnp.float32
        )
        grad_b_inner = jnp.sum(d_inner, axis=0, dtype=jnp.float32)
        d_first = d_second + jnp.einsum(
            "nf,df->nd", d_inner, w_inner, preferred_element_type=jnp.float32
        )
        d_resid, grad_gain_one, grad_shift_one = norm_one_pull(
            d_first.reshape(seqs_here, shard_rows, width)
        )
        d_attended = d_resid.astype(jnp.bfloat16)
        grad_w_output = jnp.einsum(
            "rse,srf->ef", mixed_low, d_attended, preferred_element_type=jnp.float32
        )
        grad_b_output = jnp.sum(d_attended, axis=(0, 1), dtype=jnp.float32)
        d_mixed = jnp.einsum(
            "srf,ef->rse", d_attended, w_output, preferred_element_type=jnp.float32
        ).astype(jnp.bfloat16)
        d_heads = lax.all_to_all(
            d_mixed.reshape(shard_rows, item_count, HD),
            "seq",
            split_axis=1,
            concat_axis=0,
            tiled=True,
        )
        d_query_heads, d_key_heads, d_value_heads = attention_pull(head_view(d_heads))
        returned = (
            lax.all_to_all(
                d_query_heads.astype(jnp.bfloat16), "seq", split_axis=0, concat_axis=1, tiled=True
            ),
            lax.all_to_all(
                d_key_heads.astype(jnp.bfloat16), "seq", split_axis=0, concat_axis=1, tiled=True
            ),
            lax.all_to_all(
                d_value_heads.astype(jnp.bfloat16), "seq", split_axis=0, concat_axis=1, tiled=True
            ),
        )
        d_query = returned[0].reshape(shard_rows, seqs_here, width)
        d_key = returned[1].reshape(shard_rows, seqs_here, width)
        d_value = returned[2].reshape(shard_rows, seqs_here, width)
        grad_w_query = jnp.einsum(
            "srd,rse->de", token_now, d_query, preferred_element_type=jnp.float32
        )
        grad_w_key = jnp.einsum("srd,rse->de", token_now, d_key, preferred_element_type=jnp.float32)
        grad_w_value = jnp.einsum(
            "srd,rse->de", token_now, d_value, preferred_element_type=jnp.float32
        )
        grad_b_query = jnp.sum(d_query, axis=(0, 1), dtype=jnp.float32)
        grad_b_key = jnp.sum(d_key, axis=(0, 1), dtype=jnp.float32)
        grad_b_value = jnp.sum(d_value, axis=(0, 1), dtype=jnp.float32)
        d_tokens = d_resid + jnp.einsum(
            "rse,de->srd", d_query, w_query, preferred_element_type=jnp.float32
        )
        d_tokens = d_tokens + jnp.einsum(
            "rse,de->srd", d_key, w_key, preferred_element_type=jnp.float32
        )
        d_tokens = d_tokens + jnp.einsum(
            "rse,de->srd", d_value, w_value, preferred_element_type=jnp.float32
        )
        input_grads.append(d_tokens)
        batch_grads = (
            grad_w_query,
            grad_b_query,
            grad_w_key,
            grad_b_key,
            grad_w_value,
            grad_b_value,
            grad_w_output,
            grad_b_output,
            grad_gain_one,
            grad_shift_one,
            grad_w_inner,
            grad_b_inner,
            grad_w_outer,
            grad_b_outer,
            grad_gain_two,
            grad_shift_two,
        )
        if totals is None:
            totals = batch_grads
        else:
            totals = jax.tree.map(jnp.add, totals, batch_grads)
    shards = (
        lax.psum_scatter(totals[0], ("dp", "seq"), scatter_dimension=0, tiled=True),
        lax.psum_scatter(totals[1], ("dp", "seq"), scatter_dimension=0, tiled=True),
        lax.psum_scatter(totals[2], ("dp", "seq"), scatter_dimension=0, tiled=True),
        lax.psum_scatter(totals[3], ("dp", "seq"), scatter_dimension=0, tiled=True),
        lax.psum_scatter(totals[4], ("dp", "seq"), scatter_dimension=0, tiled=True),
        lax.psum_scatter(totals[5], ("dp", "seq"), scatter_dimension=0, tiled=True),
        lax.psum_scatter(totals[6], ("dp", "seq"), scatter_dimension=0, tiled=True),
        lax.psum_scatter(totals[7], ("dp", "seq"), scatter_dimension=0, tiled=True),
        lax.psum_scatter(totals[8], ("dp", "seq"), scatter_dimension=0, tiled=True),
        lax.psum_scatter(totals[9], ("dp", "seq"), scatter_dimension=0, tiled=True),
        lax.psum_scatter(totals[10], ("dp", "seq"), scatter_dimension=0, tiled=True),
        lax.psum_scatter(totals[11], ("dp", "seq"), scatter_dimension=0, tiled=True),
        lax.psum_scatter(totals[12], ("dp", "seq"), scatter_dimension=0, tiled=True),
        lax.psum_scatter(totals[13], ("dp", "seq"), scatter_dimension=0, tiled=True),
        lax.psum_scatter(totals[14], ("dp", "seq"), scatter_dimension=0, tiled=True),
        lax.psum_scatter(totals[15], ("dp", "seq"), scatter_dimension=0, tiled=True),
    )
    return (jnp.stack(layer_rows), jnp.stack(input_grads)) + tuple(shards)


def solution(mesh):
    in_specs = (
        P(None, "dp", "seq", None),
        P(None, "dp"),
        P(("dp", "seq"), None),
        P(("dp", "seq")),
        P(("dp", "seq"), None),
        P(("dp", "seq")),
        P(("dp", "seq"), None),
        P(("dp", "seq")),
        P(("dp", "seq"), None),
        P(("dp", "seq")),
        P(("dp", "seq")),
        P(("dp", "seq")),
        P(("dp", "seq"), None),
        P(("dp", "seq")),
        P(("dp", "seq"), None),
        P(("dp", "seq")),
        P(("dp", "seq")),
        P(("dp", "seq")),
        P(None, "dp", "seq", None),
    )
    out_specs = (
        P(None, "dp", "seq", None),
        P(None, "dp", "seq", None),
        P(("dp", "seq"), None),
        P(("dp", "seq")),
        P(("dp", "seq"), None),
        P(("dp", "seq")),
        P(("dp", "seq"), None),
        P(("dp", "seq")),
        P(("dp", "seq"), None),
        P(("dp", "seq")),
        P(("dp", "seq")),
        P(("dp", "seq")),
        P(("dp", "seq"), None),
        P(("dp", "seq")),
        P(("dp", "seq"), None),
        P(("dp", "seq")),
        P(("dp", "seq")),
        P(("dp", "seq")),
    )
    return jax.shard_map(
        per_device, mesh=mesh, in_specs=in_specs, out_specs=out_specs, check_vma=False
    )
```

profile of v0, /device:TPU:0, one launch (start us, length us, event | category | flops | bytes accessed | tf_op | source)
XLA Modules:
  0.0 1656.1 jit_solution(1364522023092862360)
XLA Ops:
  19.0 42.7 %all-reduce.21 = (bf16[768]{0:T(1024)(128)(2,1)S(1)}, bf16[768]{0:T(1024)(128)(2,1)S(1)}, bf16[768]{0:T(1024)(128)(2,1)S(1)}, bf16[768]{0:T(1024)(128)(2,1)}, bf...) all-reduce(bf16[768]{0:T(1024)(128)(2,1)S(1)} %dynamic-update-slice, ...), channel_id=1, replica_groups=mesh['dp'=8,'seq'=4] {'dp','seq'}, use_global_device_ids=true, to_apply=%add | all-reduce | flops 9984 | bytes 39936
  61.6 6.1 all-gather.9.cloned.1.call-done
  74.6 53.0 %all-gather.7.cloned.1.call-done = bf16[768,768]{1,0:T(8,128)(2,1)} async-done(((bf16[24,768]{1,0:T(8,128)(2,1)}), bf16[768,768]{1,0:T(8,128)(2,1)}) %all-gather.7.cloned.1.call-update) | async-done | bytes 1179664 | tf_op jit(solution)/shard_map/all_gather | solution.py:121
  130.6 4.2 all-to-all-start.4
  134.8 52.8 %all-gather.11.cloned.1.call-done = bf16[768,768]{1,0:T(8,128)(2,1)} async-done(((bf16[24,768]{1,0:T(8,128)(2,1)}), bf16[768,768]{1,0:T(8,128)(2,1)}) %all-gather.11.cloned.1.call-update) | async-done | bytes 1179664 | tf_op jit(solution)/shard_map/all_gather | solution.py:119
  190.6 4.3 all-to-all-start.6
  196.6 19.9 %all-to-all-done.6 = bf16[512,12,64]{0,2,1:T(8,128)(2,1)} async-done(((bf16[512,12,64]{0,2,1:T(8,128)(2,1)}), bf16[512,12,64]{0,2,1:T(8,128)(2,1)}, u32[]{:S(2)}, u32[]{:S(2)}) %all-to-all-start.6) | async-done | bytes 786464 | tf_op jit(solution)/shard_map/all_to_all | solution.py:168
  223.6 17.4 %all-to-all-done.1 = bf16[512,12,64]{0,2,1:T(8,128)(2,1)S(1)} async-done(((bf16[512,12,64]{0,2,1:T(8,128)(2,1)}), bf16[512,12,64]{0,2,1:T(8,128)(2,1)S(1)}, u32[]{:S(2)}, u32[]{:S(2)}) %all-to-all-start.1) | async-done | bytes 786464 | tf_op jit(solution)/shard_map/all_to_all | solution.py:182
  254.7 11.4 all-to-all-done
  266.1 4.4 all-to-all-start.2
  274.3 109.1 %while.111 = (s32[]{:T(128)}, f32[3,64,64]{2,1,0:T(8,128)S(1)}, f32[3,64,64]{2,1,0:T(8,128)S(1)}, f32[3,64]{1,0:T(4,128)}, f32[3,64]{1,0:T(4,128)}, /*index=5*/b...) while((s32[]{:T(128)}, f32[3,64,64]{2,1,0:T(8,128)S(1)}, ...), condition=%wide.region_13.14_spmd.clone, body=%wide.region_9.13_spmd.clone.sunk | while | flops 2122035456 | bytes 35606024 | solution.py:67
  280.3 4.7 fusion.642
  307.0 4.7 fusion.642
  334.5 4.7 fusion.642
  362.0 4.8 fusion.642
  391.5 5.6 all-to-all-start.7
  402.3 92.9 %while.110 = (s32[]{:T(128)}, f32[3,64,64]{2,1,0:T(8,128)S(1)}, f32[3,64,64]{2,1,0:T(8,128)S(1)}, f32[3,64]{1,0:T(4,128)S(1)}, f32[3,64]{1,0:T(4,128)S(1)}, /*in...) while((s32[]{:T(128)}, f32[3,64,64]{2,1,0:T(8,128)S(1)}, ...), condition=%wide.region_4.5_spmd.clone, body=%wide.region_0.0_spmd.clone.sunk | while | flops 2122035456 | bytes 35605332 | solution.py:67
  500.6 5.3 all-to-all-start.3
  511.2 13.5 all-to-all-done.3
  537.9 7.0 fusion.388
  544.9 7.9 fusion.404
  557.1 4.2 fusion.402
  568.8 4.5 fusion.410
  573.3 18.0 %convert_reduce_fusion.1 = (f32[3072]{0:T(1024)}, bf16[512,3072]{1,0:T(8,128)(2,1)}, f32[3072]{0:T(1024)}, bf16[512,3072]{1,0:T(8,128)(2,1)S(1)}) fusion(f32[512,3072]{1,0:T(8,128)} %copy-done.110, f32[3072]{0:T(1024)S(1)} %convert_element_type.481, f32[512,3072]{1,0:T(8,128)} %fusion.410, f32[512,3072]{1,0:T(8,128)} %fusion.388, ...), kind=kOutput, calls=%fused_computation.463 | convolution fusion | flops 2488264704 | bytes 30707712 | tf_op jit(solution)/shard_map/nd,fd->nf/dot_general | solution.py:232
  616.4 11.5 all-to-all-done.8
  627.9 4.2 all-to-all-start.12
  636.5 173.0 %while.112 = (s32[]{:T(128)}, f32[3,64,64]{2,1,0:T(8,128)S(1)}, f32[3,64,64]{2,1,0:T(8,128)S(1)}, f32[3,64]{1,0:T(4,128)S(1)}, f32[3,64]{1,0:T(4,128)S(1)}, /*in...) while((s32[]{:T(128)}, f32[3,64,64]{2,1,0:T(8,128)S(1)}, ...), condition=%wide.region_25.26_spmd.clone, body=%wide.region_22.25_spmd.clone.sunk | while | flops 6211543040 | bytes 82320360 | solution.py:67
  814.9 5.0 all-to-all-start.11
  825.4 183.5 %while.113 = (s32[]{:T(128)}, f32[3,64,64]{2,1,0:T(8,128)S(1)}, f32[3,64,64]{2,1,0:T(8,128)S(1)}, f32[3,64]{1,0:T(4,128)S(1)}, f32[3,64]{1,0:T(4,128)S(1)}, /*in...) while((s32[]{:T(128)}, f32[3,64,64]{2,1,0:T(8,128)S(1)}, ...), condition=%wide.region_33.34_spmd.clone, body=%wide.region_30.33_spmd.clone.sunk | while | flops 6211543040 | bytes 82320360 | solution.py:67
  1014.3 5.1 all-to-all-start.15
  1024.5 13.5 all-to-all-done.15
  1055.0 4.2 reshape.1171
  1067.4 4.2 reshape.1165
  1071.6 11.5 all-to-all-done.10
  1083.1 4.2 all-to-all-start.14
  1095.4 17.3 %all-to-all-done.14 = bf16[4,2,49152]{2,1,0:T(2,128)(2,1)} async-done(((bf16[4,2,49152]{2,1,0:T(2,128)(2,1)}), bf16[4,2,49152]{2,1,0:T(2,128)(2,1)}, u32[]{:S(2)}, u32[]{:S(2)}) %all-to-all-start.14) | async-done | bytes 786464 | tf_op jit(solution)/shard_map/all_to_all | solution.py:265
  1145.0 4.2 reshape.1167
  1149.2 11.8 all-to-all-done.9
  1161.0 4.2 all-to-all-start.13
  1173.3 11.6 all-to-all-done.13
  1201.4 6.3 fusion.389
  1207.8 10.5 convolution_add_fusion.24
  1219.0 5.5 fusion.386
  1224.5 6.0 convolution_add_fusion.25
  1262.7 38.7 %all-reduce.20 = (f32[768]{0:T(1024)S(1)}, f32[768]{0:T(1024)S(1)}, f32[768]{0:T(1024)S(1)}, f32[768]{0:T(1024)S(1)}, f32[768]{0:T(1024)S(1)}, /*index=5*/f32[76...) all-reduce(f32[768]{0:T(1024)S(1)} %add.724, ...), channel_id=3, replica_groups=mesh['dp'=8,'seq'=4] {'dp','seq'}, use_global_device_ids=true, to_apply=%region_37.38.clone | all-reduce | flops 9984 | bytes 79872
  1319.1 46.5 %reduce-scatter.19.cloned.1.call-done = f32[24,768]{1,0:T(8,128)} async-done(((f32[768,768]{1,0:T(8,128)}), f32[24,768]{1,0:T(8,128)}) %reduce-scatter.19.cloned.1.call-update) | async-done | bytes 73744
  1365.5 141.8 %reduce-scatter.17.cloned.1.call-done = f32[96,768]{1,0:T(8,128)} async-done(((f32[3072,768]{1,0:T(8,128)}), f32[96,768]{1,0:T(8,128)}) %reduce-scatter.17.cloned.1.call-update) | async-done | bytes 294928 | tf_op jit(solution)/shard_map/reduce_scatter | solution.py:330
  1507.3 141.4 %reduce-scatter.15.cloned.1.call-done = f32[24,3072]{1,0:T(8,128)} async-done(((f32[768,3072]{1,0:T(8,128)}), f32[24,3072]{1,0:T(8,128)}) %reduce-scatter.15.cloned.1.call-update) | async-done | bytes 294928 | tf_op jit(solution)/shard_map/reduce_scatter | solution.py:328
  (1063 shorter events, 769.1 us)
Async XLA Ops:
  7.2 60.5 %all-gather.9.cloned.1.call-start = ((), (), s32[]{:S(2)}) async-start(), calls=%async_computation.23 | async-start | bytes 1216512 | tf_op jit(solution)/shard_map/all_gather | solution.py:123
  7.9 119.6 %all-gather.7.cloned.1.call-start = ((), (), s32[]{:S(2)}) async-start(), calls=%async_computation.22 | async-start | bytes 1216512 | tf_op jit(solution)/shard_map/all_gather | solution.py:121
  8.7 178.9 %all-gather.11.cloned.1.call-start = ((), (), s32[]{:S(2)}) async-start(), calls=%async_computation.24 | async-start | bytes 1216512 | tf_op jit(solution)/shard_map/all_gather | solution.py:119
  9.4 521.8 %all-gather.13.cloned.1.call-start = ((), (), s32[]{:S(2)}) async-start(), calls=%async_computation.25 | async-start | bytes 1216512 | tf_op jit(solution)/shard_map/all_gather | solution.py:125
  10.0 528.0 %all-gather.15.cloned.1.call-start = ((), (), s32[]{:S(2)}) async-start(), calls=%async_computation.26 | async-start | bytes 4866048 | tf_op jit(solution)/shard_map/all_gather | solution.py:129
  70.9 56.7 %copy-start.6 = (bf16[2,1,512,768]{3,2,1,0:T(8,128)(2,1)S(1)}, bf16[2,1,512,768]{3,2,1,0:T(8,128)(2,1)}, u32[]{:S(2)}) copy-start(bf16[2,1,512,768]{3,2,1,0:T(8,128)(2,1)} %param.27) | copy-start | bytes 4718596
  70.9 59.6 %all-to-all-start.5 = ((bf16[512,12,64]{0,2,1:T(8,128)(2,1)}), bf16[512,12,64]{0,2,1:T(8,128)(2,1)S(1)}, u32[]{:S(2)}, u32[]{:S(2)}) async-start(bf16[512,12,64]{0,2,1:T(8,128)(2,1)} %bitcast.37), calls=%async_computation.5 | async-start | bytes 1572864 | tf_op jit(solution)/shard_map/all_to_all | solution.py:182
  130.6 57.0 %copy-start.33 = (bf16[512,12,64]{0,2,1:T(8,128)(2,1)}, bf16[512,12,64]{0,2,1:T(8,128)(2,1)S(1)}, u32[]{:S(2)}) copy-start(bf16[512,12,64]{0,2,1:T(8,128)(2,1)S(1)} %all-to-all-done.5) | copy-start | bytes 2359300
  130.6 60.0 %all-to-all-start.4 = ((bf16[512,12,64]{0,2,1:T(8,128)(2,1)}), bf16[512,12,64]{0,2,1:T(8,128)(2,1)}, u32[]{:S(2)}, u32[]{:S(2)}) async-start(bf16[512,12,64]{0,2,1:T(8,128)(2,1)} %bitcast.32), calls=%async_computation.4 | async-start | bytes 1572864 | tf_op jit(solution)/shard_map/all_to_all | solution.py:175
  190.6 26.0 %all-to-all-start.6 = ((bf16[512,12,64]{0,2,1:T(8,128)(2,1)}), bf16[512,12,64]{0,2,1:T(8,128)(2,1)}, u32[]{:S(2)}, u32[]{:S(2)}) async-start(bf16[512,12,64]{0,2,1:T(8,128)(2,1)} %bitcast.1129), calls=%async_computation.6 | async-start | bytes 1572864 | tf_op jit(solution)/shard_map/all_to_all | solution.py:168
  216.5 24.5 %all-to-all-start.1 = ((bf16[512,12,64]{0,2,1:T(8,128)(2,1)}), bf16[512,12,64]{0,2,1:T(8,128)(2,1)S(1)}, u32[]{:S(2)}, u32[]{:S(2)}) async-start(bf16[512,12,64]{0,2,1:T(8,128)(2,1)} %bitcast.1128), calls=%async_computation.1 | async-start | bytes 1572864 | tf_op jit(solution)/shard_map/all_to_all | solution.py:182
  220.0 324.9 %all-gather.17.cloned.1.call-start = ((), (), s32[]{:S(2)}) async-start(), calls=%async_computation.27 | async-start | bytes 4866048 | tf_op jit(solution)/shard_map/all_gather | solution.py:131
  223.6 20.9 %copy-start.102 = (s32[2,1]{0,1:T(1,128)S(1)}, s32[2,1]{0,1:T(1,128)}, u32[]{:S(2)}) copy-start(s32[2,1]{0,1:T(1,128)} %param.28) | copy-start | bytes 28
  241.0 25.1 %all-to-all-start = ((bf16[512,12,64]{0,2,1:T(8,128)(2,1)}), bf16[512,12,64]{0,2,1:T(8,128)(2,1)S(1)}, u32[]{:S(2)}, u32[]{:S(2)}) async-start(bf16[512,12,64]{0,2,1:T(8,128)(2,1)} %bitcast.1127), calls=%async_computation | async-start | bytes 1572864 | tf_op jit(solution)/shard_map/all_to_all | solution.py:175
  266.1 125.5 %all-to-all-start.2 = ((bf16[512,12,64]{0,2,1:T(8,128)(2,1)}), bf16[512,12,64]{0,2,1:T(8,128)(2,1)}, u32[]{:S(2)}, u32[]{:S(2)}) async-start(bf16[512,12,64]{0,2,1:T(8,128)(2,1)} %bitcast.14), calls=%async_computation.2 | async-start | bytes 1572864 | tf_op jit(solution)/shard_map/all_to_all | solution.py:168
  286.7 8.4 copy-start.36
  313.5 9.1 copy-start
  313.5 9.1 copy-start.36
  340.9 9.1 copy-start
  340.9 9.1 copy-start.36
  368.4 9.1 copy-start
  368.4 9.1 copy-start.36
  391.5 109.1 %all-to-all-start.7 = ((bf16[4,2,49152]{2,1,0:T(2,128)(2,1)}), bf16[4,2,49152]{2,1,0:T(2,128)(2,1)}, u32[]{:S(2)}, u32[]{:S(2)}) async-start(bf16[4,2,49152]{2,1,0:T(2,128)(2,1)} %reshape.1161), calls=%async_computation.7 | async-start | bytes 1572864 | tf_op jit(solution)/shard_map/all_to_all | solution.py:199
  500.6 24.1 %all-to-all-start.3 = ((bf16[4,2,49152]{2,1,0:T(2,128)(2,1)}), bf16[4,2,49152]{2,1,0:T(2,128)(2,1)S(1)}, u32[]{:S(2)}, u32[]{:S(2)}) async-start(bf16[4,2,49152]{2,1,0:T(2,128)(2,1)} %reshape.1163), calls=%async_computation.3 | async-start | bytes 1572864 | tf_op jit(solution)/shard_map/all_to_all | solution.py:199
  506.0 92.5 %copy-start.64 = (f32[768]{0:T(1024)}, f32[768]{0:T(1024)S(1)}, u32[]{:S(2)}) copy-start(f32[768]{0:T(1024)S(1)} %convert_element_type.478) | copy-start | bytes 9220
  506.0 51.0 %copy-start.66 = (f32[768]{0:T(1024)}, f32[768]{0:T(1024)S(1)}, u32[]{:S(2)}) copy-start(f32[768]{0:T(1024)S(1)} %convert_element_type.479) | copy-start | bytes 9220
  506.1 67.3 %copy-start.86 = (f32[3072]{0:T(1024)}, f32[3072]{0:T(1024)S(1)}, u32[]{:S(2)}) copy-start(f32[3072]{0:T(1024)S(1)} %convert_element_type.481) | copy-start | bytes 36868
  533.8 64.8 %copy-start.4 = (f32[1,512,768]{2,1,0:T(8,128)}, f32[1,512,768]{2,1,0:T(8,128)S(1)}, u32[]{:S(2)}) copy-start(f32[1,512,768]{2,1,0:T(8,128)S(1)} %get-tuple-element.1720) | copy-start | bytes 4718596
  533.8 64.7 %copy-start.68 = (f32[512]{0:T(512)}, f32[512]{0:T(512)S(1)}, u32[]{:S(2)}) copy-start(f32[512]{0:T(512)S(1)} %broadcast_multiply_fusion.5) | copy-start | bytes 6148
  536.4 62.1 %copy-start.74 = (f32[512]{0:T(512)}, f32[512]{0:T(512)S(1)}, u32[]{:S(2)}) copy-start(f32[512]{0:T(512)S(1)} %broadcast_multiply_fusion.7) | copy-start | bytes 6148
  537.9 60.7 %copy-start.72 = (f32[512]{0:T(512)}, f32[512]{0:T(512)S(1)}, u32[]{:S(2)}) copy-start(f32[512]{0:T(512)S(1)} %fusion.384) | copy-start | bytes 6148
  537.9 60.7 %copy-start.90 = (f32[512]{0:T(512)}, f32[512]{0:T(512)S(1)}, u32[]{:S(2)}) copy-start(f32[512]{0:T(512)S(1)} %fusion.382) | copy-start | bytes 6148
  599.9 8.4 copy-start.11
  600.0 8.4 copy-start.76
  604.8 23.1 %all-to-all-start.8 = ((bf16[512,12,64]{0,2,1:T(8,128)(2,1)}), bf16[512,12,64]{0,2,1:T(8,128)(2,1)S(1)}, u32[]{:S(2)}, u32[]{:S(2)}) async-start(bf16[512,12,64]{0,2,1:T(8,128)(2,1)} %bitcast.66), calls=%async_computation.8 | async-start | bytes 1572864 | tf_op jit(solution)/shard_map/all_to_all | solution.py:253
  608.3 710.8 %reduce-scatter.13.cloned.1.call-start = ((), (), s32[]{:S(2)}) async-start(), calls=%async_computation.28 | async-start | bytes 2433024 | tf_op jit(solution)/shard_map/reduce_scatter | solution.py:324
  627.9 187.0 %all-to-all-start.12 = ((bf16[512,12,64]{0,2,1:T(8,128)(2,1)}), bf16[512,12,64]{0,2,1:T(8,128)(2,1)}, u32[]{:S(2)}, u32[]{:S(2)}) async-start(bf16[512,12,64]{0,2,1:T(8,128)(2,1)} %bitcast.104), calls=%async_computation.12 | async-start | bytes 1572864 | tf_op jit(solution)/shard_map/all_to_all | solution.py:253
  814.9 199.4 %all-to-all-start.11 = ((bf16[4,2,49152]{2,1,0:T(2,128)(2,1)}), bf16[4,2,49152]{2,1,0:T(2,128)(2,1)}, u32[]{:S(2)}, u32[]{:S(2)}) async-start(bf16[4,2,49152]{2,1,0:T(2,128)(2,1)} %reshape.1175), calls=%async_computation.11 | async-start | bytes 1572864 | tf_op jit(solution)/shard_map/all_to_all | solution.py:268
  1014.3 23.6 %all-to-all-start.15 = ((bf16[4,2,49152]{2,1,0:T(2,128)(2,1)}), bf16[4,2,49152]{2,1,0:T(2,128)(2,1)S(1)}, u32[]{:S(2)}, u32[]{:S(2)}) async-start(bf16[4,2,49152]{2,1,0:T(2,128)(2,1)} %reshape.1169), calls=%async_computation.15 | async-start | bytes 1572864 | tf_op jit(solution)/shard_map/all_to_all | solution.py:268
  1019.4 299.7 %reduce-scatter.23.cloned.1.call-start = ((), (), s32[]{:S(2)}) async-start(), calls=%async_computation.33 | async-start | bytes 2433024
  1059.2 23.9 %all-to-all-start.10 = ((bf16[4,2,49152]{2,1,0:T(2,128)(2,1)}), bf16[4,2,49152]{2,1,0:T(2,128)(2,1)}, u32[]{:S(2)}, u32[]{:S(2)}) async-start(bf16[4,2,49152]{2,1,0:T(2,128)(2,1)} %reshape.1171), calls=%async_computation.10 | async-start | bytes 1572864 | tf_op jit(solution)/shard_map/all_to_all | solution.py:265
  1083.1 29.6 %all-to-all-start.14 = ((bf16[4,2,49152]{2,1,0:T(2,128)(2,1)}), bf16[4,2,49152]{2,1,0:T(2,128)(2,1)}, u32[]{:S(2)}, u32[]{:S(2)}) async-start(bf16[4,2,49152]{2,1,0:T(2,128)(2,1)} %reshape.1165), calls=%async_computation.14 | async-start | bytes 1572864 | tf_op jit(solution)/shard_map/all_to_all | solution.py:265
  1087.3 231.7 %reduce-scatter.21.cloned.1.call-start = ((), (), s32[]{:S(2)}) async-start(), calls=%async_computation.32 | async-start | bytes 2433024
  1136.8 24.2 %all-to-all-start.9 = ((bf16[4,2,49152]{2,1,0:T(2,128)(2,1)}), bf16[4,2,49152]{2,1,0:T(2,128)(2,1)}, u32[]{:S(2)}, u32[]{:S(2)}) async-start(bf16[4,2,49152]{2,1,0:T(2,128)(2,1)} %reshape.1173), calls=%async_computation.9 | async-start | bytes 1572864 | tf_op jit(solution)/shard_map/all_to_all | solution.py:262
  1161.0 24.0 %all-to-all-start.13 = ((bf16[4,2,49152]{2,1,0:T(2,128)(2,1)}), bf16[4,2,49152]{2,1,0:T(2,128)(2,1)}, u32[]{:S(2)}, u32[]{:S(2)}) async-start(bf16[4,2,49152]{2,1,0:T(2,128)(2,1)} %reshape.1167), calls=%async_computation.13 | async-start | bytes 1572864 | tf_op jit(solution)/shard_map/all_to_all | solution.py:262
  1165.2 200.3 %reduce-scatter.19.cloned.1.call-start = ((), (), s32[]{:S(2)}) async-start(), calls=%async_computation.31 | async-start | bytes 2433024
  1200.7 306.5 %reduce-scatter.17.cloned.1.call-start = ((), (), s32[]{:S(2)}) async-start(), calls=%async_computation.30 | async-start | bytes 9732096 | tf_op jit(solution)/shard_map/reduce_scatter | solution.py:330
  1218.3 430.4 %reduce-scatter.15.cloned.1.call-start = ((), (), s32[]{:S(2)}) async-start(), calls=%async_computation.29 | async-start | bytes 9732096 | tf_op jit(solution)/shard_map/reduce_scatter | solution.py:328
  (154 other events, 483.9 us)
Sparse Core Ops, SparseCore 0:
  10.8 56.8 all-gather.8
  70.5 57.0 all-gather.6
  130.4 57.1 all-gather.10
  190.2 65.9 all-gather.12
  258.8 71.8 all-gather.14
  333.3 61.7 all-gather.16
  615.0 100.7 reduce-scatter.12
  1051.0 100.6 reduce-scatter.22
  1157.6 103.5 reduce-scatter.20
  1266.9 98.6 reduce-scatter.18
  1372.0 135.2 reduce-scatter.16
  1513.6 135.0 reduce-scatter.14
where the time goes:
time: 1670 us; the launch traced here: 1660 us
  waiting for transfers between devices  585 us (35%)
  matrix products  537 us (32%)
  local copies, waits for them, and re-layouts  221 us (13%)
  other arithmetic  86.3 us (5%)
  blocking collectives  81.3 us (5%)
  starting transfers between devices  69.6 us (4%)
  loops' own time  60.4 us (4%)
    reduce_scatter x1, waiting for transfers between devices, per_device(): lax.psum_scatter(totals[12], ('dp', 'seq'), scatter_dimension=0, tiled=True)  142 us
    reduce_scatter x1, waiting for transfers between devices, per_device(): lax.psum_scatter(totals[10], ('dp', 'seq'), scatter_dimension=0, tiled=True)  141 us
    dot_general x32, matrix products, attend(): jnp.einsum('igd,jgd->gij', query_sin, key_sin, precision=highest)  107 us
    dot_general x32, matrix products, attend(): scores = jnp.einsum('igd,jgd->gij', query_cos, key_cos, precision=highest)  99.1 us
    unnamed x237, local copies, waits for them, and re-layouts  89.4 us
    unnamed x2, blocking collectives  81.3 us
    dot_general x32, matrix products, attend(): numer = jnp.einsum('gij,jge->ige', scores, value_blk, precision=highest)  79.1 us
    another operation x4, loops' own time, attention(): final_state, outputs = lax.scan(jax.checkpoint(attend), initial, stacked)  60.4 us
  transfers between devices with their start and end apart: 28, of which 16 were waited for; matrix products, arithmetic and copies ran while one was open for 47% of the time, Pallas kernels for 0%

commit v1 on v0

--- a/solution.py
+++ b/solution.py
@@ -259,8 +259,17 @@
         )
         d_query_heads, d_key_heads, d_value_heads = attention_pull(head_view(d_heads))
         returned = (
-            lax.all_to_all(
-                d_query_heads.astype(jnp.bfloat16), "seq", split_axis=0, concat_axis=1, tiled=True
+            jnp.concatenate(
+                lax.all_to_all(
+                    jnp.stack(
+                        jnp.split(d_query_heads.astype(jnp.bfloat16), lax.axis_size("seq"), axis=0),
+                        axis=0,
+                    ),
+                    "seq",
+                    0,
+                    0,
+                ),
+                axis=1,
             ),
             lax.all_to_all(
                 d_key_heads.astype(jnp.bfloat16), "seq", split_axis=0, concat_axis=1, tiled=True

time: 1670 us -> 1660 us (level)
  local copies, waits for them, and re-layouts: 221 us -> 181 us
  blocking collectives: 81.3 us -> 105 us
    all_to_all x0 -> x1, blocking collectives: none -> 24.6 us  [per_device(): lax.all_to_all(jnp.stack(jnp.split(d_query_heads.astype(jnp.bfloat16), la...]
    unnamed x237 -> x227, local copies, waits for them, and re-layouts: 89.4 us -> 71.2 us
    unnamed x15, waiting for transfers between devices: 50.2 us -> 68.4 us
  transfers between devices with their start and end apart: 28 -> 27, of which waited for: 16 -> 15; matrix products, arithmetic and copies ran while one was open for 47% -> 45% of each run, Pallas kernels for 0% -> 0%
where the time goes in v1:
time: 1660 us; the launch traced here: 1650 us
  waiting for transfers between devices  595 us (36%)
  matrix products  542 us (33%)
  local copies, waits for them, and re-layouts  181 us (11%)
  blocking collectives  105 us (6%)
  other arithmetic  86.3 us (5%)
  starting transfers between devices  65.3 us (4%)
  loops' own time  59 us (4%)
    reduce_scatter x1, waiting for transfers between devices, per_device(): lax.psum_scatter(totals[12], ('dp', 'seq'), scatter_dimension=0, tiled=True)  142 us
    reduce_scatter x1, waiting for transfers between devices, per_device(): lax.psum_scatter(totals[10], ('dp', 'seq'), scatter_dimension=0, tiled=True)  141 us
    dot_general x32, matrix products, attend(): jnp.einsum('igd,jgd->gij', query_sin, key_sin, precision=highest)  107 us
    dot_general x32, matrix products, attend(): scores = jnp.einsum('igd,jgd->gij', query_cos, key_cos, precision=highest)  99.1 us
    unnamed x2, blocking collectives  80.8 us
    dot_general x32, matrix products, attend(): numer = jnp.einsum('gij,jge->ige', scores, value_blk, precision=highest)  79.1 us
    unnamed x227, local copies, waits for them, and re-layouts  71.2 us
    unnamed x15, waiting for transfers between devices  68.4 us
  transfers between devices with their start and end apart: 27, of which 15 were waited for; matrix products, arithmetic and copies ran while one was open for 45% of the time, Pallas kernels for 0%

profile of v1, /device:TPU:0, one launch (start us, length us, event | category | flops | bytes accessed | tf_op | source)
XLA Modules:
  0.0 1650.3 jit_solution(3359227789678907376)
XLA Ops:
  19.0 42.7 %all-reduce.21 = (bf16[768]{0:T(1024)(128)(2,1)S(1)}, bf16[768]{0:T(1024)(128)(2,1)S(1)}, bf16[768]{0:T(1024)(128)(2,1)S(1)}, bf16[768]{0:T(1024)(128)(2,1)}, bf...) all-reduce(bf16[768]{0:T(1024)(128)(2,1)S(1)} %dynamic-update-slice, ...), channel_id=1, replica_groups=mesh['dp'=8,'seq'=4] {'dp','seq'}, use_global_device_ids=true, to_apply=%add | all-reduce | flops 9984 | bytes 39936
  61.7 6.0 all-gather.9.cloned.1.call-done
  74.6 52.9 %all-gather.7.cloned.1.call-done = bf16[768,768]{1,0:T(8,128)(2,1)} async-done(((bf16[24,768]{1,0:T(8,128)(2,1)}), bf16[768,768]{1,0:T(8,128)(2,1)}) %all-gather.7.cloned.1.call-update) | async-done | bytes 1179664 | tf_op jit(solution)/shard_map/all_gather | solution.py:121
  134.7 52.8 %all-gather.11.cloned.1.call-done = bf16[768,768]{1,0:T(8,128)(2,1)} async-done(((bf16[24,768]{1,0:T(8,128)(2,1)}), bf16[768,768]{1,0:T(8,128)(2,1)}) %all-gather.11.cloned.1.call-update) | async-done | bytes 1179664 | tf_op jit(solution)/shard_map/all_gather | solution.py:119
  190.5 4.3 all-to-all-start.6
  196.6 19.9 %all-to-all-done.6 = bf16[512,12,64]{0,2,1:T(8,128)(2,1)} async-done(((bf16[512,12,64]{0,2,1:T(8,128)(2,1)}), bf16[512,12,64]{0,2,1:T(8,128)(2,1)}, u32[]{:S(2)}, u32[]{:S(2)}) %all-to-all-start.6) | async-done | bytes 786464 | tf_op jit(solution)/shard_map/all_to_all | solution.py:168
  223.6 17.3 %all-to-all-done.1 = bf16[512,12,64]{0,2,1:T(8,128)(2,1)S(1)} async-done(((bf16[512,12,64]{0,2,1:T(8,128)(2,1)}), bf16[512,12,64]{0,2,1:T(8,128)(2,1)S(1)}, u32[]{:S(2)}, u32[]{:S(2)}) %all-to-all-start.1) | async-done | bytes 786464 | tf_op jit(solution)/shard_map/all_to_all | solution.py:182
  254.6 11.3 all-to-all-done
  266.0 4.4 all-to-all-start.2
  274.2 109.7 %while.111 = (s32[]{:T(128)}, f32[3,64,64]{2,1,0:T(8,128)S(1)}, f32[3,64,64]{2,1,0:T(8,128)S(1)}, f32[3,64]{1,0:T(4,128)}, f32[3,64]{1,0:T(4,128)}, /*index=5*/b...) while((s32[]{:T(128)}, f32[3,64,64]{2,1,0:T(8,128)S(1)}, ...), condition=%wide.region_13.14_spmd.clone, body=%wide.region_9.13_spmd.clone.sunk | while | flops 2122035456 | bytes 35606024 | solution.py:67
  280.2 4.7 fusion.642
  307.1 4.7 fusion.642
  334.7 4.7 fusion.642
  362.2 4.7 fusion.642
  392.0 5.5 all-to-all-start.7
  402.7 92.9 %while.110 = (s32[]{:T(128)}, f32[3,64,64]{2,1,0:T(8,128)S(1)}, f32[3,64,64]{2,1,0:T(8,128)S(1)}, f32[3,64]{1,0:T(4,128)S(1)}, f32[3,64]{1,0:T(4,128)S(1)}, /*in...) while((s32[]{:T(128)}, f32[3,64,64]{2,1,0:T(8,128)S(1)}, ...), condition=%wide.region_4.5_spmd.clone, body=%wide.region_0.0_spmd.clone.sunk | while | flops 2122035456 | bytes 35605332 | solution.py:67
  501.0 5.3 all-to-all-start.3
  511.6 13.5 all-to-all-done.3
  538.4 7.0 fusion.388
  545.4 7.9 fusion.404
  557.5 4.2 fusion.402
  569.2 4.5 fusion.410
  573.7 18.0 %convert_reduce_fusion.1 = (f32[3072]{0:T(1024)}, bf16[512,3072]{1,0:T(8,128)(2,1)}, f32[3072]{0:T(1024)}, bf16[512,3072]{1,0:T(8,128)(2,1)S(1)}) fusion(f32[512,3072]{1,0:T(8,128)} %copy-done.107, f32[3072]{0:T(1024)S(1)} %convert_element_type.477, f32[512,3072]{1,0:T(8,128)} %fusion.410, f32[512,3072]{1,0:T(8,128)} %fusion.388, ...), kind=kOutput, calls=%fused_computation.463 | convolution fusion | flops 2488264704 | bytes 30707712 | tf_op jit(solution)/shard_map/nd,fd->nf/dot_general | solution.py:232
  616.8 11.5 all-to-all-done.8
  628.3 4.2 all-to-all-start.12
  636.9 173.0 %while.112 = (s32[]{:T(128)}, f32[3,64,64]{2,1,0:T(8,128)S(1)}, f32[3,64,64]{2,1,0:T(8,128)S(1)}, f32[3,64]{1,0:T(4,128)S(1)}, f32[3,64]{1,0:T(4,128)S(1)}, /*in...) while((s32[]{:T(128)}, f32[3,64,64]{2,1,0:T(8,128)S(1)}, ...), condition=%wide.region_25.26_spmd.clone, body=%wide.region_22.25_spmd.clone.sunk | while | flops 6211543040 | bytes 82320360 | solution.py:67
  815.2 5.1 all-to-all-start.11
  825.8 182.2 %while.113 = (s32[]{:T(128)}, f32[3,64,64]{2,1,0:T(8,128)S(1)}, f32[3,64,64]{2,1,0:T(8,128)S(1)}, f32[3,64]{1,0:T(4,128)S(1)}, f32[3,64]{1,0:T(4,128)S(1)}, /*in...) while((s32[]{:T(128)}, f32[3,64,64]{2,1,0:T(8,128)S(1)}, ...), condition=%wide.region_33.34_spmd.clone, body=%wide.region_30.33_spmd.clone.sunk | while | flops 6211543040 | bytes 82320360 | solution.py:67
  1013.3 5.1 all-to-all-start.15
  1023.5 13.5 all-to-all-done.15
  1054.0 4.2 reshape.1189
  1066.5 4.2 reshape.1185
  1070.7 11.5 all-to-all-done.10
  1094.5 17.4 %all-to-all-done.14 = bf16[4,2,49152]{2,1,0:T(2,128)(2,1)} async-done(((bf16[4,2,49152]{2,1,0:T(2,128)(2,1)}), bf16[4,2,49152]{2,1,0:T(2,128)(2,1)}, u32[]{:S(2)}, u32[]{:S(2)}) %all-to-all-start.14) | async-done | bytes 786464 | tf_op jit(solution)/shard_map/all_to_all | solution.py:274
  1127.8 24.6 %all_to_all.172 = bf16[4,512,3,64]{1,3,2,0:T(8,128)(2,1)} all-to-all(bf16[4,512,3,64]{1,3,2,0:T(8,128)(2,1)} %get-tuple-element.1058), channel_id=1, replica_groups=mesh['dp'=8,'seq'=4] {'seq'}, dimensions={0} | all-to-all | bytes 1572864 | tf_op jit(solution)/shard_map/all_to_all | solution.py:263
  1152.4 4.2 all-to-all-start.13
  1160.3 15.5 all-to-all-done.13
  1175.8 4.5 add_bitcast_fusion.2
  1184.0 6.4 fusion.389
  1190.4 10.3 convolution_add_fusion.24
  1201.5 5.7 fusion.386
  1207.2 6.1 convolution_add_fusion.25
  1221.7 4.2 copy.342
  1231.6 4.3 copy.339
  1239.7 38.0 %all-reduce.20 = (f32[768]{0:T(1024)S(1)}, f32[768]{0:T(1024)S(1)}, f32[768]{0:T(1024)S(1)}, f32[768]{0:T(1024)S(1)}, f32[768]{0:T(1024)S(1)}, /*index=5*/f32[76...) all-reduce(f32[768]{0:T(1024)S(1)} %add.724, ...), channel_id=3, replica_groups=mesh['dp'=8,'seq'=4] {'dp','seq'}, use_global_device_ids=true, to_apply=%region_37.38.clone | all-reduce | flops 9984 | bytes 79872
  1294.8 64.7 %reduce-scatter.19.cloned.1.call-done = f32[24,768]{1,0:T(8,128)} async-done(((f32[768,768]{1,0:T(8,128)}), f32[24,768]{1,0:T(8,128)}) %reduce-scatter.19.cloned.1.call-update) | async-done | bytes 73744
  1359.5 142.0 %reduce-scatter.17.cloned.1.call-done = f32[96,768]{1,0:T(8,128)} async-done(((f32[3072,768]{1,0:T(8,128)}), f32[96,768]{1,0:T(8,128)}) %reduce-scatter.17.cloned.1.call-update) | async-done | bytes 294928 | tf_op jit(solution)/shard_map/reduce_scatter | solution.py:339
  1501.5 141.4 %reduce-scatter.15.cloned.1.call-done = f32[24,3072]{1,0:T(8,128)} async-done(((f32[768,3072]{1,0:T(8,128)}), f32[24,3072]{1,0:T(8,128)}) %reduce-scatter.15.cloned.1.call-update) | async-done | bytes 294928 | tf_op jit(solution)/shard_map/reduce_scatter | solution.py:337
  (1045 shorter events, 729.6 us)
Async XLA Ops:
  7.2 60.5 %all-gather.9.cloned.1.call-start = ((), (), s32[]{:S(2)}) async-start(), calls=%async_computation.23 | async-start | bytes 1216512 | tf_op jit(solution)/shard_map/all_gather | solution.py:123
  7.9 119.6 %all-gather.7.cloned.1.call-start = ((), (), s32[]{:S(2)}) async-start(), calls=%async_computation.22 | async-start | bytes 1216512 | tf_op jit(solution)/shard_map/all_gather | solution.py:121
  8.7 178.8 %all-gather.11.cloned.1.call-start = ((), (), s32[]{:S(2)}) async-start(), calls=%async_computation.24 | async-start | bytes 1216512 | tf_op jit(solution)/shard_map/all_gather | solution.py:119
  9.4 522.3 %all-gather.13.cloned.1.call-start = ((), (), s32[]{:S(2)}) async-start(), calls=%async_computation.25 | async-start | bytes 1216512 | tf_op jit(solution)/shard_map/all_gather | solution.py:125
  10.0 528.4 %all-gather.15.cloned.1.call-start = ((), (), s32[]{:S(2)}) async-start(), calls=%async_computation.26 | async-start | bytes 4866048 | tf_op jit(solution)/shard_map/all_gather | solution.py:129
  70.9 56.6 %copy-start.5 = (bf16[2,1,512,768]{3,2,1,0:T(8,128)(2,1)S(1)}, bf16[2,1,512,768]{3,2,1,0:T(8,128)(2,1)}, u32[]{:S(2)}) copy-start(bf16[2,1,512,768]{3,2,1,0:T(8,128)(2,1)} %param.27) | copy-start | bytes 4718596
  70.9 59.6 %all-to-all-start.5 = ((bf16[512,12,64]{0,2,1:T(8,128)(2,1)}), bf16[512,12,64]{0,2,1:T(8,128)(2,1)S(1)}, u32[]{:S(2)}, u32[]{:S(2)}) async-start(bf16[512,12,64]{0,2,1:T(8,128)(2,1)} %bitcast.37), calls=%async_computation.5 | async-start | bytes 1572864 | tf_op jit(solution)/shard_map/all_to_all | solution.py:182
  130.5 57.0 %copy-start.34 = (bf16[512,12,64]{0,2,1:T(8,128)(2,1)}, bf16[512,12,64]{0,2,1:T(8,128)(2,1)S(1)}, u32[]{:S(2)}) copy-start(bf16[512,12,64]{0,2,1:T(8,128)(2,1)S(1)} %all-to-all-done.5) | copy-start | bytes 2359300
  130.5 60.0 %all-to-all-start.4 = ((bf16[512,12,64]{0,2,1:T(8,128)(2,1)}), bf16[512,12,64]{0,2,1:T(8,128)(2,1)}, u32[]{:S(2)}, u32[]{:S(2)}) async-start(bf16[512,12,64]{0,2,1:T(8,128)(2,1)} %bitcast.32), calls=%async_computation.4 | async-start | bytes 1572864 | tf_op jit(solution)/shard_map/all_to_all | solution.py:175
  190.5 26.0 %all-to-all-start.6 = ((bf16[512,12,64]{0,2,1:T(8,128)(2,1)}), bf16[512,12,64]{0,2,1:T(8,128)(2,1)}, u32[]{:S(2)}, u32[]{:S(2)}) async-start(bf16[512,12,64]{0,2,1:T(8,128)(2,1)} %bitcast.1115), calls=%async_computation.6 | async-start | bytes 1572864 | tf_op jit(solution)/shard_map/all_to_all | solution.py:168
  216.5 24.4 %all-to-all-start.1 = ((bf16[512,12,64]{0,2,1:T(8,128)(2,1)}), bf16[512,12,64]{0,2,1:T(8,128)(2,1)S(1)}, u32[]{:S(2)}, u32[]{:S(2)}) async-start(bf16[512,12,64]{0,2,1:T(8,128)(2,1)} %bitcast.1114), calls=%async_computation.1 | async-start | bytes 1572864 | tf_op jit(solution)/shard_map/all_to_all | solution.py:182
  220.0 325.4 %all-gather.17.cloned.1.call-start = ((), (), s32[]{:S(2)}) async-start(), calls=%async_computation.27 | async-start | bytes 4866048 | tf_op jit(solution)/shard_map/all_gather | solution.py:131
  223.6 20.9 %copy-start.99 = (s32[2,1]{0,1:T(1,128)S(1)}, s32[2,1]{0,1:T(1,128)}, u32[]{:S(2)}) copy-start(s32[2,1]{0,1:T(1,128)} %param.28) | copy-start | bytes 28
  240.9 25.1 %all-to-all-start = ((bf16[512,12,64]{0,2,1:T(8,128)(2,1)}), bf16[512,12,64]{0,2,1:T(8,128)(2,1)S(1)}, u32[]{:S(2)}, u32[]{:S(2)}) async-start(bf16[512,12,64]{0,2,1:T(8,128)(2,1)} %bitcast.1113), calls=%async_computation | async-start | bytes 1572864 | tf_op jit(solution)/shard_map/all_to_all | solution.py:175
  266.0 126.0 %all-to-all-start.2 = ((bf16[512,12,64]{0,2,1:T(8,128)(2,1)}), bf16[512,12,64]{0,2,1:T(8,128)(2,1)}, u32[]{:S(2)}, u32[]{:S(2)}) async-start(bf16[512,12,64]{0,2,1:T(8,128)(2,1)} %bitcast.14), calls=%async_computation.2 | async-start | bytes 1572864 | tf_op jit(solution)/shard_map/all_to_all | solution.py:168
  286.7 8.4 copy-start
  286.7 8.4 copy-start.37
  313.6 9.2 copy-start
  313.6 9.2 copy-start.37
  341.1 9.2 copy-start
  341.2 9.2 copy-start.37
  368.7 9.3 copy-start
  368.7 9.3 copy-start.37
  392.0 109.0 %all-to-all-start.7 = ((bf16[4,2,49152]{2,1,0:T(2,128)(2,1)}), bf16[4,2,49152]{2,1,0:T(2,128)(2,1)}, u32[]{:S(2)}, u32[]{:S(2)}) async-start(bf16[4,2,49152]{2,1,0:T(2,128)(2,1)} %reshape.1181), calls=%async_computation.7 | async-start | bytes 1572864 | tf_op jit(solution)/shard_map/all_to_all | solution.py:199
  501.0 24.2 %all-to-all-start.3 = ((bf16[4,2,49152]{2,1,0:T(2,128)(2,1)}), bf16[4,2,49152]{2,1,0:T(2,128)(2,1)S(1)}, u32[]{:S(2)}, u32[]{:S(2)}) async-start(bf16[4,2,49152]{2,1,0:T(2,128)(2,1)} %reshape.1183), calls=%async_computation.3 | async-start | bytes 1572864 | tf_op jit(solution)/shard_map/all_to_all | solution.py:199
  506.4 92.6 %copy-start.61 = (f32[768]{0:T(1024)}, f32[768]{0:T(1024)S(1)}, u32[]{:S(2)}) copy-start(f32[768]{0:T(1024)S(1)} %convert_element_type.474) | copy-start | bytes 9220
  506.4 51.1 %copy-start.63 = (f32[768]{0:T(1024)}, f32[768]{0:T(1024)S(1)}, u32[]{:S(2)}) copy-start(f32[768]{0:T(1024)S(1)} %convert_element_type.475) | copy-start | bytes 9220
  506.4 67.3 %copy-start.83 = (f32[3072]{0:T(1024)}, f32[3072]{0:T(1024)S(1)}, u32[]{:S(2)}) copy-start(f32[3072]{0:T(1024)S(1)} %convert_element_type.477) | copy-start | bytes 36868
  534.2 64.7 %copy-start.3 = (f32[1,512,768]{2,1,0:T(8,128)}, f32[1,512,768]{2,1,0:T(8,128)S(1)}, u32[]{:S(2)}) copy-start(f32[1,512,768]{2,1,0:T(8,128)S(1)} %get-tuple-element.1720) | copy-start | bytes 4718596
  534.3 64.7 %copy-start.65 = (f32[512]{0:T(512)}, f32[512]{0:T(512)S(1)}, u32[]{:S(2)}) copy-start(f32[512]{0:T(512)S(1)} %broadcast_multiply_fusion.5) | copy-start | bytes 6148
  536.9 62.1 %copy-start.71 = (f32[512]{0:T(512)}, f32[512]{0:T(512)S(1)}, u32[]{:S(2)}) copy-start(f32[512]{0:T(512)S(1)} %broadcast_multiply_fusion.7) | copy-start | bytes 6148
  538.3 60.7 %copy-start.69 = (f32[512]{0:T(512)}, f32[512]{0:T(512)S(1)}, u32[]{:S(2)}) copy-start(f32[512]{0:T(512)S(1)} %fusion.384) | copy-start | bytes 6148
  538.4 60.6 %copy-start.87 = (f32[512]{0:T(512)}, f32[512]{0:T(512)S(1)}, u32[]{:S(2)}) copy-start(f32[512]{0:T(512)S(1)} %fusion.382) | copy-start | bytes 6148
  600.4 8.4 copy-start.9
  605.2 23.1 %all-to-all-start.8 = ((bf16[512,12,64]{0,2,1:T(8,128)(2,1)}), bf16[512,12,64]{0,2,1:T(8,128)(2,1)S(1)}, u32[]{:S(2)}, u32[]{:S(2)}) async-start(bf16[512,12,64]{0,2,1:T(8,128)(2,1)} %bitcast.66), calls=%async_computation.8 | async-start | bytes 1572864 | tf_op jit(solution)/shard_map/all_to_all | solution.py:253
  608.7 686.1 %reduce-scatter.13.cloned.1.call-start = ((), (), s32[]{:S(2)}) async-start(), calls=%async_computation.28 | async-start | bytes 2433024 | tf_op jit(solution)/shard_map/reduce_scatter | solution.py:333
  628.3 187.0 %all-to-all-start.12 = ((bf16[512,12,64]{0,2,1:T(8,128)(2,1)}), bf16[512,12,64]{0,2,1:T(8,128)(2,1)}, u32[]{:S(2)}, u32[]{:S(2)}) async-start(bf16[512,12,64]{0,2,1:T(8,128)(2,1)} %bitcast.101), calls=%async_computation.12 | async-start | bytes 1572864 | tf_op jit(solution)/shard_map/all_to_all | solution.py:253
  815.2 198.1 %all-to-all-start.11 = ((bf16[4,2,49152]{2,1,0:T(2,128)(2,1)}), bf16[4,2,49152]{2,1,0:T(2,128)(2,1)}, u32[]{:S(2)}, u32[]{:S(2)}) async-start(bf16[4,2,49152]{2,1,0:T(2,128)(2,1)} %reshape.1191), calls=%async_computation.11 | async-start | bytes 1572864 | tf_op jit(solution)/shard_map/all_to_all | solution.py:277
  1013.3 23.6 %all-to-all-start.15 = ((bf16[4,2,49152]{2,1,0:T(2,128)(2,1)}), bf16[4,2,49152]{2,1,0:T(2,128)(2,1)S(1)}, u32[]{:S(2)}, u32[]{:S(2)}) async-start(bf16[4,2,49152]{2,1,0:T(2,128)(2,1)} %reshape.1187), calls=%async_computation.15 | async-start | bytes 1572864 | tf_op jit(solution)/shard_map/all_to_all | solution.py:277
  1018.4 276.4 %reduce-scatter.23.cloned.1.call-start = ((), (), s32[]{:S(2)}) async-start(), calls=%async_computation.33 | async-start | bytes 2433024
  1058.2 23.9 %all-to-all-start.10 = ((bf16[4,2,49152]{2,1,0:T(2,128)(2,1)}), bf16[4,2,49152]{2,1,0:T(2,128)(2,1)}, u32[]{:S(2)}, u32[]{:S(2)}) async-start(bf16[4,2,49152]{2,1,0:T(2,128)(2,1)} %reshape.1189), calls=%async_computation.10 | async-start | bytes 1572864 | tf_op jit(solution)/shard_map/all_to_all | solution.py:274
  1082.1 29.8 %all-to-all-start.14 = ((bf16[4,2,49152]{2,1,0:T(2,128)(2,1)}), bf16[4,2,49152]{2,1,0:T(2,128)(2,1)}, u32[]{:S(2)}, u32[]{:S(2)}) async-start(bf16[4,2,49152]{2,1,0:T(2,128)(2,1)} %reshape.1185), calls=%async_computation.14 | async-start | bytes 1572864 | tf_op jit(solution)/shard_map/all_to_all | solution.py:274
  1086.3 208.5 %reduce-scatter.21.cloned.1.call-start = ((), (), s32[]{:S(2)}) async-start(), calls=%async_computation.32 | async-start | bytes 2433024
  1152.4 23.3 %all-to-all-start.13 = ((bf16[4,512,3,64]{1,3,2,0:T(8,128)(2,1)}), bf16[4,512,3,64]{1,3,2,0:T(8,128)(2,1)}, u32[]{:S(2)}, u32[]{:S(2)}) async-start(bf16[4,512,3,64]{1,3,2,0:T(8,128)(2,1)} %get-tuple-element.1065), calls=%async_computation.13 | async-start | bytes 1572864 | tf_op jit(solution)/shard_map/all_to_all | solution.py:263
  1156.6 202.9 %reduce-scatter.19.cloned.1.call-start = ((), (), s32[]{:S(2)}) async-start(), calls=%async_computation.31 | async-start | bytes 2433024
  1183.3 318.2 %reduce-scatter.17.cloned.1.call-start = ((), (), s32[]{:S(2)}) async-start(), calls=%async_computation.30 | async-start | bytes 9732096 | tf_op jit(solution)/shard_map/reduce_scatter | solution.py:339
  1200.8 442.2 %reduce-scatter.15.cloned.1.call-start = ((), (), s32[]{:S(2)}) async-start(), calls=%async_computation.29 | async-start | bytes 9732096 | tf_op jit(solution)/shard_map/reduce_scatter | solution.py:337
  1236.3 47.3 %copy-start.49 = (bf16[512,4,3,64]{0,3,2,1:T(8,128)(2,1)S(1)}, bf16[512,4,3,64]{0,3,2,1:T(8,128)(2,1)}, u32[]{:S(2)}) copy-start(bf16[512,4,3,64]{0,3,2,1:T(8,128)(2,1)} %copy.257) | copy-start | bytes 2359300
  (150 other events, 477.8 us)
Sparse Core Ops, SparseCore 0:
  10.8 56.8 all-gather.8
  70.5 56.9 all-gather.6
  130.3 57.1 all-gather.10
  190.2 65.8 all-gather.12
  258.7 71.9 all-gather.14
  333.3 61.8 all-gather.16
  615.3 100.2 reduce-scatter.12
  1050.0 100.7 reduce-scatter.22
  1156.7 98.4 reduce-scatter.20
  1260.9 98.5 reduce-scatter.18
  1366.0 135.4 reduce-scatter.16
  1507.9 135.0 reduce-scatter.14
